TPU v7x, 32 devices: a whole 2x2x4 slice. The times are simulated.
32 devices in a mesh: grp: 2 (over y), seq: 4 (over z), head: 2 (over x), sub: 2 (over core).
Axes of the slice: x: 2, y: 2, z: 4, core: 2. Of those that a mesh axis runs over, the one named last changes fastest.
Arguments:
- vid_q: bfloat16 [2560, 4096], P(('grp', 'seq', 'sub'), 'head'), parts along dimension 0, may hold values from -6 to 6
- vid_k: bfloat16 [2560, 4096], P(('grp', 'seq', 'sub'), 'head'), parts along dimension 0, may hold values from -6 to 6
- vid_v: bfloat16 [2560, 4096], P(('grp', 'seq', 'sub'), 'head'), parts along dimension 0, may hold values from -6 to 6
- aud_q: bfloat16 [640, 2048], P(('grp', 'seq', 'sub'), 'head'), parts along dimension 0, may hold values from -6 to 6
- cross_k: bfloat16 [2560, 2048], P(('grp', 'seq', 'sub'), 'head'), parts along dimension 0, may hold values from -6 to 6
- cross_v: bfloat16 [2560, 2048], P(('grp', 'seq', 'sub'), 'head'), parts along dimension 0, may hold values from -6 to 6
- cross_q: bfloat16 [2560, 2048], P(('grp', 'seq', 'sub'), 'head'), parts along dimension 0, may hold values from -6 to 6
- aud_k: bfloat16 [640, 2048], P(('grp', 'seq', 'sub'), 'head'), parts along dimension 0, may hold values from -6 to 6
- aud_v: bfloat16 [640, 2048], P(('grp', 'seq', 'sub'), 'head'), parts along dimension 0, may hold values from -6 to 6
- windows: int32 [2, 80], P(None, 'grp'), parts along dimension 1, may hold values from 0 to 40, as said below
Outputs:
- video_self: bfloat16 [2560, 4096], P(('grp', 'seq', 'sub'), 'head'), parts along dimension 0
- audio_out: bfloat16 [640, 2048], P(('grp', 'seq', 'sub'), 'head'), parts along dimension 0
- video_cross: bfloat16 [2560, 2048], P(('grp', 'seq', 'sub'), 'head'), parts along dimension 0
There are 2 independent parts, one for each index of `grp`. A program takes and returns all parts, laid end to end along the dimension named above; each array names one. Nothing has to cross between parts.
Inputs may be any that keep to these rules, and one draw needn't show every extreme that they name: For every stretch c, windows[0, c] lies between max(0, c - 5) and c, and windows[1, c] between c + 1 and min(40, c + 6); in every draw some stretch reaches 5 tiles on both sides.
All inputs are finite; a program needn't handle non-finite values.
Results may differ from a plain program's by a relative error of at most 0.03.
Values may be sent and summed in bfloat16 or wider, within the bound.
A program may use at most 64 MiB of HBM per device.

v0:
```python
from functools import partial
import math
import jax
import jax.numpy as jnp
from jax import lax
from jax.sharding import PartitionSpec as P

HEAD_DIM = 128
AUDIO_DIM = 64
TILE_LEN = 32
STRETCH_LEN = 8


def extended(cells, sides, width):
    for axis, dim in sides:
        count = lax.axis_size(axis)
        ends = count - 1
        head = lax.slice_in_dim(cells, 0, width, axis=dim)
        tail = lax.slice_in_dim(cells, cells.shape[dim] - width, cells.shape[dim], axis=dim)
        cells = jnp.concatenate(
            [
                lax.ppermute(tail, axis, [(i, (i + 1) % count) for i in range(ends)]),
                cells,
                lax.ppermute(head, axis, [((i + 1) % count, i) for i in range(ends)]),
            ],
            axis=dim,
        )
    return cells


def start_state(query_count, head_count, head_size):
    running = jnp.full((head_count, query_count), -jnp.inf, jnp.float32)
    summed = jnp.zeros((head_count, query_count), jnp.float32)
    numerator = jnp.zeros((head_count, query_count, head_size), jnp.float32)
    return (running, summed, numerator)


def absorb(state_in, queries, key_rows, value_rows, head_count, scaling, visible):
    running, summed, numerator = state_in
    query_count = queries.shape[0]
    key_count = key_rows.shape[0]
    head_size = queries.shape[1] // head_count
    scores = (
        jnp.einsum(
            "qhe,khe->hqk",
            queries.reshape(query_count, head_count, head_size),
            key_rows.reshape(key_count, head_count, head_size),
            preferred_element_type=jnp.float32,
        )
        * scaling
    )
    if visible is not None:
        scores = jnp.where(visible[None], scores, jnp.float32(-1e30))
    newest = jnp.maximum(running, jnp.max(scores, axis=2))
    shrink = jnp.exp(running - newest)
    weights = jnp.exp(scores - newest[:, :, None])
    summed = summed * shrink + jnp.sum(weights, axis=2)
    numerator = numerator * shrink[:, :, None] + jnp.einsum(
        "hqk,khe->hqe",
        weights.astype(jnp.bfloat16),
        value_rows.reshape(key_count, head_count, head_size),
        preferred_element_type=jnp.float32,
    )
    return (newest, summed, numerator)


def block_split(total_rows):
    block_rows = total_rows
    while block_rows > 512 and block_rows % 2 == 0:
        block_rows = block_rows // 2
    return (block_rows, total_rows // block_rows)


def fold_keys(state_in, shards_in, offset, queries, head_count, scaling):
    key_rows, value_rows = shards_in
    block_rows, block_count = block_split(key_rows.shape[0])
    key_blocks = key_rows.reshape(block_count, block_rows, key_rows.shape[1])
    value_blocks = value_rows.reshape(block_count, block_rows, value_rows.shape[1])

    def one_block(state, paired):
        return (absorb(state, queries, paired[0], paired[1], head_count, scaling, None), None)

    result, unused = lax.scan(one_block, state_in, (key_blocks, value_blocks))
    return result


def normalize_heads(state_in):
    running, summed, numerator = state_in
    mixed = numerator / summed[:, :, None]
    return mixed.transpose(1, 0, 2).reshape(mixed.shape[1], -1).astype(jnp.bfloat16)


def body(vid_q, vid_k, vid_v, aud_q, cross_k, cross_v, cross_q, aud_k, aud_v, windows):
    video_heads = vid_q.shape[1] // HEAD_DIM
    video_scaling = 1.0 / math.sqrt(HEAD_DIM)
    audio_heads = aud_q.shape[1] // AUDIO_DIM
    audio_scaling = 1.0 / math.sqrt(AUDIO_DIM)
    moved_q, moved_k, moved_v = (
        lax.all_to_all(vid_q, "sub", split_axis=1, concat_axis=0, tiled=True),
        lax.all_to_all(vid_k, "sub", split_axis=1, concat_axis=0, tiled=True),
        lax.all_to_all(vid_v, "sub", split_axis=1, concat_axis=0, tiled=True),
    )
    pair_heads = video_heads // lax.axis_size("sub")
    folder = partial(fold_keys, queries=moved_q, head_count=pair_heads, scaling=video_scaling)
    state = folder(
        start_state(moved_q.shape[0], pair_heads, HEAD_DIM),
        (
            lax.all_gather(moved_k, "seq", axis=0, tiled=True),
            lax.all_gather(moved_v, "seq", axis=0, tiled=True),
        ),
        jnp.int32(0),
    )
    video_self = lax.all_to_all(
        normalize_heads(state), "sub", split_axis=0, concat_axis=1, tiled=True
    )
    folder = partial(fold_keys, queries=aud_q, head_count=audio_heads, scaling=audio_scaling)
    state = folder(
        start_state(aud_q.shape[0], audio_heads, AUDIO_DIM),
        (
            lax.all_gather(cross_k, ("seq", "sub"), axis=0, tiled=True),
            lax.all_gather(cross_v, ("seq", "sub"), axis=0, tiled=True),
        ),
        jnp.int32(0),
    )
    audio_out = normalize_heads(state)
    audio_rows = aud_k.shape[0]
    key_width = aud_k.shape[1]
    padded_rows = extended(
        jnp.concatenate((aud_k, aud_v), axis=1), ((("seq", "sub"), 0),), audio_rows
    )
    near_keys = padded_rows[:, :key_width]
    near_values = padded_rows[:, key_width:]
    position = lax.axis_index(("seq", "sub"))
    audio_index = (position - 1) * audio_rows + jnp.arange(padded_rows.shape[0], dtype=jnp.int32)
    stretch_index = audio_index // STRETCH_LEN
    stretch_ids = jnp.arange(windows.shape[1], dtype=jnp.int32)
    onehot = stretch_index[:, None] == stretch_ids[None, :]
    first_tile = jnp.sum(jnp.where(onehot, windows[0][None, :], 0), axis=1)
    after_tile = jnp.sum(jnp.where(onehot, windows[1][None, :], 0), axis=1)
    video_rows = cross_q.shape[0]
    video_tile = (position * video_rows + jnp.arange(video_rows, dtype=jnp.int32)) // TILE_LEN
    visible = (first_tile[None, :] <= video_tile[:, None]) & (
        video_tile[:, None] < after_tile[None, :]
    )
    state = absorb(
        start_state(video_rows, audio_heads, AUDIO_DIM),
        cross_q,
        near_keys,
        near_values,
        audio_heads,
        audio_scaling,
        visible,
    )
    video_cross = normalize_heads(state)
    return (video_self, audio_out, video_cross)


def solution(mesh):
    return jax.shard_map(
        body,
        mesh=mesh,
        in_specs=(
            P(("grp", "seq", "sub"), "head"),
            P(("grp", "seq", "sub"), "head"),
            P(("grp", "seq", "sub"), "head"),
            P(("grp", "seq", "sub"), "head"),
            P(("grp", "seq", "sub"), "head"),
            P(("grp", "seq", "sub"), "head"),
            P(("grp", "seq", "sub"), "head"),
            P(("grp", "seq", "sub"), "head"),
            P(("grp", "seq", "sub"), "head"),
            P(None, "grp"),
        ),
        out_specs=(
            P(("grp", "seq", "sub"), "head"),
            P(("grp", "seq", "sub"), "head"),
            P(("grp", "seq", "sub"), "head"),
        ),
        check_vma=False,
    )
```

profile of v0, /device:TPU:0, one launch (start us, length us, event | category | flops | bytes accessed | tf_op | source)
XLA Modules:
  0.0 218.2 jit_solution(4391640885050590359)
XLA Ops:
  7.2 1.1 copy.138
  8.4 5.1 %all_to_all.73 = bf16[160,2,1024]{2,0,1:T(8,128)(2,1)} all-to-all(bf16[160,2,1024]{2,0,1:T(8,128)(2,1)S(1)} %bitcast.132), channel_id=1, replica_groups=mesh['grp'=2,'seq'=4,'head'=2,'sub'=2] {'sub'}, dimensions={1} | all-to-all | bytes 1310720 | tf_op jit(solution)/shard_map/all_to_all | solution.py:100
  13.7 5.1 %all_to_all.74 = bf16[160,2,1024]{2,0,1:T(8,128)(2,1)} all-to-all(bf16[160,2,1024]{2,0,1:T(8,128)(2,1)S(1)} %bitcast.133), channel_id=1, replica_groups=mesh['grp'=2,'seq'=4,'head'=2,'sub'=2] {'sub'}, dimensions={1} | all-to-all | bytes 1310720 | tf_op jit(solution)/shard_map/all_to_all | solution.py:101
  18.9 0.7 all-gather.9.cloned.1.call-update
  19.6 1.3 collective-permute-start.1
  20.9 3.7 %collective-permute-start = (bf16[40,2048]{1,0:T(8,128)(2,1)S(1)}, bf16[40,2048]{1,0:T(8,128)(2,1)}, u32[]{:S(2)}, u32[]{:S(2)}) collective-permute-start(bf16[40,2048]{1,0:T(8,128)(2,1)S(1)} %constant_dynamic-update-slice_fusion), channel_id=1, source_target_pairs={{0,1},{1,4},{4,5},{5,8},{8,9},{9,12},{12,13},{2,3},{3,6},{6,7},{7,... | collective-permute-start | bytes 491528 | tf_op jit(solution)/shard_map/ppermute | solution.py:22
  24.6 0.9 copy.137
  25.5 3.6 %all-to-all-start.1 = ((bf16[160,2,1024]{2,0,1:T(8,128)(2,1)}), bf16[160,2,1024]{2,0,1:T(8,128)(2,1)S(1)}, u32[]{:S(2)}, u32[]{:S(2)}) async-start(bf16[160,2,1024]{2,0,1:T(8,128)(2,1)} %bitcast.94), calls=%async_computation.1 | async-start | bytes 1310720 | tf_op jit(solution)/shard_map/all_to_all | solution.py:99
  29.2 0.5 all-gather.11.cloned.1.call-update
  30.3 1.0 pad_maximum_fusion
  31.4 0.8 copy.104
  32.4 0.9 fusion.37
  33.3 1.0 fusion.29
  34.3 0.6 fusion.28
  35.0 0.9 copy.105
  35.9 36.1 %all-gather.5.cloned.1.call-done = bf16[1280,1024]{1,0:T(8,128)(2,1)} async-done(((bf16[320,1024]{1,0:T(8,128)(2,1)}), bf16[1280,1024]{1,0:T(8,128)(2,1)}) %all-gather.5.cloned.1.call-update) | async-done | bytes 2621456 | tf_op jit(solution)/shard_map/all_gather | solution.py:108
  72.0 55.8 %all-gather.7.cloned.1.call-done = bf16[1280,1024]{1,0:T(8,128)(2,1)} async-done(((bf16[320,1024]{1,0:T(8,128)(2,1)}), bf16[1280,1024]{1,0:T(8,128)(2,1)}) %all-gather.7.cloned.1.call-update) | async-done | bytes 2621456 | tf_op jit(solution)/shard_map/all_gather | solution.py:109
  127.8 35.4 %while.30 = (s32[]{:T(128)}, f32[8,320]{1,0:T(8,128)S(1)}, f32[8,320]{1,0:T(8,128)S(1)}, f32[8,320,128]{2,1,0:T(8,128)S(1)}, bf16[4,320,1024]{2,1,0:T(8,128)(2,1...) while((s32[]{:T(128)}, f32[8,320]{1,0:T(8,128)S(1)}, ...), condition=%wide.region_3.4_spmd.clone, body=%wide.region_0.3_spmd.clone.sunk | while | flops 426979840 | bytes 32931984 | solution.py:83
  127.8 1.4 dynamic-slice_bitcast_fusion.3
  129.3 2.5 %bitcast_reduce_fusion.2 = (f32[8,320]{1,0:T(8,128)S(1)}, f32[8,320,320]{2,1,0:T(8,128)}) fusion(bf16[320,8,128]{2,1,0:T(8,128)(2,1)S(1)} %bitcast.123, bf16[320,1024]{1,0:T(8,128)(2,1)S(1)} %get-tuple-element.365), kind=kOutput, calls=%fused_computation.1.clone.1 | convolution fusion | flops 211351040 | bytes 4597760 | tf_op jit(solution)/shard_map/while/body/eval_jaxpr/qhe,khe->hqk/dot_general | solution.py:44
  131.8 3.0 %fusion.59 = f32[8,320]{1,0:T(8,128)S(1)} fusion(f32[8,320,320]{2,1,0:T(8,128)} %get-tuple-element.325, f32[8,320]{1,0:T(8,128)S(1)} %select_maximum_fusion.4), kind=kLoop, calls=%fused_computation.4.clone.1 | loop fusion | flops 2455040 | bytes 3297280 | tf_op jit(solution)/shard_map/while/body/eval_jaxpr/reduce_sum | solution.py:57
  135.2 1.4 fusion.61
  136.6 1.4 dynamic-slice_bitcast_fusion.3
  138.1 2.5 %bitcast_reduce_fusion.2 = (f32[8,320]{1,0:T(8,128)S(1)}, f32[8,320,320]{2,1,0:T(8,128)}) fusion(bf16[320,8,128]{2,1,0:T(8,128)(2,1)S(1)} %bitcast.123, bf16[320,1024]{1,0:T(8,128)(2,1)S(1)} %get-tuple-element.365), kind=kOutput, calls=%fused_computation.1.clone.1 | convolution fusion | flops 211351040 | bytes 4597760 | tf_op jit(solution)/shard_map/while/body/eval_jaxpr/qhe,khe->hqk/dot_general | solution.py:44
  140.7 3.0 %fusion.59 = f32[8,320]{1,0:T(8,128)S(1)} fusion(f32[8,320,320]{2,1,0:T(8,128)} %get-tuple-element.325, f32[8,320]{1,0:T(8,128)S(1)} %select_maximum_fusion.4), kind=kLoop, calls=%fused_computation.4.clone.1 | loop fusion | flops 2455040 | bytes 3297280 | tf_op jit(solution)/shard_map/while/body/eval_jaxpr/reduce_sum | solution.py:57
  144.0 1.4 fusion.61
  145.5 1.4 dynamic-slice_bitcast_fusion.3
  147.0 2.5 %bitcast_reduce_fusion.2 = (f32[8,320]{1,0:T(8,128)S(1)}, f32[8,320,320]{2,1,0:T(8,128)}) fusion(bf16[320,8,128]{2,1,0:T(8,128)(2,1)S(1)} %bitcast.123, bf16[320,1024]{1,0:T(8,128)(2,1)S(1)} %get-tuple-element.365), kind=kOutput, calls=%fused_computation.1.clone.1 | convolution fusion | flops 211351040 | bytes 4597760 | tf_op jit(solution)/shard_map/while/body/eval_jaxpr/qhe,khe->hqk/dot_general | solution.py:44
  149.5 3.0 %fusion.59 = f32[8,320]{1,0:T(8,128)S(1)} fusion(f32[8,320,320]{2,1,0:T(8,128)} %get-tuple-element.325, f32[8,320]{1,0:T(8,128)S(1)} %select_maximum_fusion.4), kind=kLoop, calls=%fused_computation.4.clone.1 | loop fusion | flops 2455040 | bytes 3297280 | tf_op jit(solution)/shard_map/while/body/eval_jaxpr/reduce_sum | solution.py:57
  152.9 1.4 fusion.61
  154.3 1.4 dynamic-slice_bitcast_fusion.3
  155.9 2.5 %bitcast_reduce_fusion.2 = (f32[8,320]{1,0:T(8,128)S(1)}, f32[8,320,320]{2,1,0:T(8,128)}) fusion(bf16[320,8,128]{2,1,0:T(8,128)(2,1)S(1)} %bitcast.123, bf16[320,1024]{1,0:T(8,128)(2,1)S(1)} %get-tuple-element.365), kind=kOutput, calls=%fused_computation.1.clone.1 | convolution fusion | flops 211351040 | bytes 4597760 | tf_op jit(solution)/shard_map/while/body/eval_jaxpr/qhe,khe->hqk/dot_general | solution.py:44
  158.4 3.0 %fusion.59 = f32[8,320]{1,0:T(8,128)S(1)} fusion(f32[8,320,320]{2,1,0:T(8,128)} %get-tuple-element.325, f32[8,320]{1,0:T(8,128)S(1)} %select_maximum_fusion.4), kind=kLoop, calls=%fused_computation.4.clone.1 | loop fusion | flops 2455040 | bytes 3297280 | tf_op jit(solution)/shard_map/while/body/eval_jaxpr/reduce_sum | solution.py:57
  161.7 1.4 fusion.61
  163.6 0.4 copy.97
  164.3 4.4 %all_to_all.75 = bf16[2,160,1024]{2,1,0:T(8,128)(2,1)S(1)} all-to-all(bf16[2,160,1024]{2,1,0:T(8,128)(2,1)S(1)} %convert_element_type.36), channel_id=1, replica_groups=mesh['grp'=2,'seq'=4,'head'=2,'sub'=2] {'sub'}, dimensions={0} | all-to-all | bytes 1310720 | tf_op jit(solution)/shard_map/all_to_all | solution.py:113
  168.7 0.9 copy.116
  169.6 26.7 %all-gather.11.cloned.1.call-done = bf16[1280,1024]{1,0:T(8,128)(2,1)} async-done(((bf16[160,1024]{1,0:T(8,128)(2,1)}), bf16[1280,1024]{1,0:T(8,128)(2,1)}) %all-gather.11.cloned.1.call-update) | async-done | bytes 2621456 | tf_op jit(solution)/shard_map/all_gather | solution.py:121
  196.3 14.4 %while.31 = (s32[]{:T(128)}, f32[16,40]{1,0:T(8,128)S(1)}, f32[16,40]{1,0:T(8,128)S(1)}, f32[16,40,64]{2,1,0:T(8,128)S(1)}, bf16[4,320,1024]{2,1,0:T(8,128)(2,1)...) while((s32[]{:T(128)}, f32[16,40]{1,0:T(8,128)S(1)}, ...), condition=%wide.region_7.8_spmd.clone, body=%wide.region_4.7_spmd.clone.sunk | while | flops 53783680 | bytes 9625717 | solution.py:83
  196.3 1.4 constant_dynamic-slice_fusion.3
  199.4 0.5 convolution_add_fusion.2
  199.9 1.4 constant_dynamic-slice_fusion.3
  203.0 0.5 convolution_add_fusion.2
  203.5 1.4 constant_dynamic-slice_fusion.3
  206.6 0.5 convolution_add_fusion.2
  207.1 1.4 constant_dynamic-slice_fusion.3
  210.2 0.5 convolution_add_fusion.2
  210.9 0.8 convert_element_type.39
  (109 shorter events, 10.3 us)
Async XLA Ops:
  7.2 64.8 %all-gather.5.cloned.1.call-start = ((), (), s32[]{:S(2)}) async-start(), calls=%async_computation.4 | async-start | bytes 3276800 | tf_op jit(solution)/shard_map/all_gather | solution.py:108
  8.3 5.2 %copy-start.2 = (bf16[160,2048]{1,0:T(8,128)(2,1)S(1)}, bf16[160,2048]{1,0:T(8,128)(2,1)}, u32[]{:S(2)}) copy-start(bf16[160,2048]{1,0:T(8,128)(2,1)} %param.16) | copy-start | bytes 1966084
  13.5 114.2 %all-gather.7.cloned.1.call-start = ((), (), s32[]{:S(2)}) async-start(), calls=%async_computation.5 | async-start | bytes 3276800 | tf_op jit(solution)/shard_map/all_gather | solution.py:109
  13.6 5.9 %copy-start.6 = (bf16[40,1024]{1,0:T(8,128)(2,1)S(1)}, bf16[40,1024]{1,0:T(8,128)(2,1)}, u32[]{:S(2)}) copy-start(bf16[40,1024]{1,0:T(8,128)(2,1)} %param.21) | copy-start | bytes 245764
  13.7 6.0 %copy-start.7 = (bf16[40,1024]{1,0:T(8,128)(2,1)S(1)}, bf16[40,1024]{1,0:T(8,128)(2,1)}, u32[]{:S(2)}) copy-start(bf16[40,1024]{1,0:T(8,128)(2,1)} %param.22) | copy-start | bytes 245764
  13.7 11.0 %copy-start.3 = (bf16[160,2048]{1,0:T(8,128)(2,1)S(1)}, bf16[160,2048]{1,0:T(8,128)(2,1)}, u32[]{:S(2)}) copy-start(bf16[160,2048]{1,0:T(8,128)(2,1)} %param.14) | copy-start | bytes 1966084
  18.8 150.8 %all-gather.9.cloned.1.call-start = ((), (), s32[]{:S(2)}) async-start(), calls=%async_computation.6 | async-start | bytes 2949120 | tf_op jit(solution)/shard_map/all_gather | solution.py:120
  19.6 10.7 %collective-permute-start.1 = (bf16[40,2048]{1,0:T(8,128)(2,1)S(1)}, bf16[40,2048]{1,0:T(8,128)(2,1)}, u32[]{:S(2)}, u32[]{:S(2)}) collective-permute-start(bf16[40,2048]{1,0:T(8,128)(2,1)S(1)} %constant_dynamic-update-slice_fusion), channel_id=1, source_target_pairs={{1,0},{4,1},{5,4},{8,5},{9,8},{12,9},{13,12},{3,2},{6,3},{7,6},{10... | collective-permute-start | bytes 491528 | tf_op jit(solution)/shard_map/ppermute | solution.py:24
  20.9 9.4 %collective-permute-start = (bf16[40,2048]{1,0:T(8,128)(2,1)S(1)}, bf16[40,2048]{1,0:T(8,128)(2,1)}, u32[]{:S(2)}, u32[]{:S(2)}) collective-permute-start(bf16[40,2048]{1,0:T(8,128)(2,1)S(1)} %constant_dynamic-update-slice_fusion), channel_id=1, source_target_pairs={{0,1},{1,4},{4,5},{5,8},{8,9},{9,12},{12,13},{2,3},{3,6},{6,7},{7,... | collective-permute-start | bytes 491528 | tf_op jit(solution)/shard_map/ppermute | solution.py:22
  24.6 5.2 %copy-start.4 = (bf16[160,1024]{1,0:T(8,128)(2,1)S(1)}, bf16[160,1024]{1,0:T(8,128)(2,1)}, u32[]{:S(2)}) copy-start(bf16[160,1024]{1,0:T(8,128)(2,1)} %param.20) | copy-start | bytes 983044
  25.5 4.5 %copy-start.8 = (s32[2,40]{1,0:T(2,128)S(1)}, s32[2,40]{1,0:T(2,128)}, u32[]{:S(2)}) copy-start(s32[2,40]{1,0:T(2,128)} %param.23) | copy-start | bytes 964
  25.5 10.4 %all-to-all-start.1 = ((bf16[160,2,1024]{2,0,1:T(8,128)(2,1)}), bf16[160,2,1024]{2,0,1:T(8,128)(2,1)S(1)}, u32[]{:S(2)}, u32[]{:S(2)}) async-start(bf16[160,2,1024]{2,0,1:T(8,128)(2,1)} %bitcast.94), calls=%async_computation.1 | async-start | bytes 1310720 | tf_op jit(solution)/shard_map/all_to_all | solution.py:99
  29.2 167.1 %all-gather.11.cloned.1.call-start = ((), (), s32[]{:S(2)}) async-start(), calls=%async_computation.7 | async-start | bytes 2949120 | tf_op jit(solution)/shard_map/all_gather | solution.py:121
  32.4 1.9 copy-start.5
  131.8 3.4 %copy-start = (f32[8,320,320]{2,1,0:T(8,128)S(1)}, f32[8,320,320]{2,1,0:T(8,128)}, u32[]{:S(2)}) copy-start(f32[8,320,320]{2,1,0:T(8,128)} %get-tuple-element.325) | copy-start | bytes 9830404 | tf_op jit(solution)/shard_map/while
  140.7 3.4 %copy-start = (f32[8,320,320]{2,1,0:T(8,128)S(1)}, f32[8,320,320]{2,1,0:T(8,128)}, u32[]{:S(2)}) copy-start(f32[8,320,320]{2,1,0:T(8,128)} %get-tuple-element.325) | copy-start | bytes 9830404 | tf_op jit(solution)/shard_map/while
  149.5 3.4 %copy-start = (f32[8,320,320]{2,1,0:T(8,128)S(1)}, f32[8,320,320]{2,1,0:T(8,128)}, u32[]{:S(2)}) copy-start(f32[8,320,320]{2,1,0:T(8,128)} %get-tuple-element.325) | copy-start | bytes 9830404 | tf_op jit(solution)/shard_map/while
  158.4 3.3 %copy-start = (f32[8,320,320]{2,1,0:T(8,128)S(1)}, f32[8,320,320]{2,1,0:T(8,128)}, u32[]{:S(2)}) copy-start(f32[8,320,320]{2,1,0:T(8,128)} %get-tuple-element.325) | copy-start | bytes 9830404 | tf_op jit(solution)/shard_map/while
  164.3 32.0 %copy-start.1 = (bf16[40,1024]{1,0:T(8,128)(2,1)S(1)}, bf16[40,1024]{1,0:T(8,128)(2,1)}, u32[]{:S(2)}) copy-start(bf16[40,1024]{1,0:T(8,128)(2,1)} %param.17) | copy-start | bytes 245764
Sparse Core Ops, SparseCore 0:
  13.6 58.2 all-gather.4
  73.6 54.1 all-gather.6
  129.4 32.4 all-gather.8
  163.4 32.8 all-gather.10
where the time goes:
time: 219 us; the launch traced here: 218 us
  waiting for transfers between devices  120 us (55%)
  local copies, waits for them, and re-layouts  23.1 us (11%)
  matrix products  20.8 us (9%)
  other arithmetic  16.4 us (7%)
  blocking collectives  14.7 us (7%)
  between operations  14.1 us (6%)
  starting transfers between devices  8.81 us (4%)
    all_gather x1, waiting for transfers between devices, body(): lax.all_gather(moved_v, 'seq', axis=0, tiled=True)  55.8 us
    all_gather x1, waiting for transfers between devices, body(): lax.all_gather(moved_k, 'seq', axis=0, tiled=True)  36.1 us
    all_gather x1, waiting for transfers between devices, body(): lax.all_gather(cross_v, ('seq', 'sub'), axis=0, tiled=True)  26.7 us
    reduce_sum x9, other arithmetic, absorb(): summed = summed * shrink + jnp.sum(weights, axis=2)  14.4 us
    dot_general x9, matrix products, absorb(): jnp.einsum('qhe,khe->hqk', queries.reshape(query_count, head_count, head_...  12.6 us
    dynamic_slice x12, local copies, waits for them, and re-layouts, fold_keys(): result, unused = lax.scan(one_block, state_in, (key_blocks, value_blocks))  8.35 us
    dot_general x9, matrix products, absorb(): jnp.einsum('hqk,khe->hqe', weights.astype(jnp.bfloat16), value_rows.resha...  8.23 us
    while x28, local copies, waits for them, and re-layouts  7.43 us
  transfers between devices with their start and end apart: 7, of which 3 were waited for; matrix products, arithmetic and copies ran while one was open for 20% of the time, Pallas kernels for 0%

commit v1 on v0

--- a/solution.py
+++ b/solution.py
@@ -105,7 +105,9 @@
     state = folder(
         start_state(moved_q.shape[0], pair_heads, HEAD_DIM),
         (
-            lax.all_gather(moved_k, "seq", axis=0, tiled=True),
+            jnp.concatenate(
+                lax.all_to_all(jnp.stack([moved_k] * lax.axis_size("seq")), "seq", 0, 0), axis=0
+            ),
             lax.all_gather(moved_v, "seq", axis=0, tiled=True),
         ),
         jnp.int32(0),

time: 219 us -> 208 us (0.950)
  waiting for transfers between devices: 120 us -> 101 us
  starting transfers between devices: 8.81 us -> 15.1 us
    all_to_all x1 -> x2, waiting for transfers between devices: 0.01 us -> 84.2 us  [the longest x1 82.4 us: body(): lax.all_to_all(jnp.stack([moved_k] * lax.axis_size('seq')), 'seq', 0, 0)]
    all_gather x1, waiting for transfers between devices: 55.8 us -> 0.01 us  [body(): lax.all_gather(moved_v, 'seq', axis=0, tiled=True)]
    all_gather x1 -> x0, waiting for transfers between devices: 36.1 us -> none  [body(): lax.all_gather(moved_k, 'seq', axis=0, tiled=True)]
    all_gather x1, waiting for transfers between devices: 26.7 us -> 16.1 us  [body(): lax.all_gather(cross_v, ('seq', 'sub'), axis=0, tiled=True)]
    all_to_all x1 -> x2, starting transfers between devices: 3.64 us -> 9.99 us  [the longest x1 6.48 us: body(): lax.all_to_all(jnp.stack([moved_k] * lax.axis_size('seq')), 'seq', 0, 0)]
  transfers between devices with their start and end apart: 7 -> 7, of which waited for: 3 -> 3; matrix products, arithmetic and copies ran while one was open for 20% -> 22% of each run, Pallas kernels for 0% -> 0%
where the time goes in v1:
time: 208 us; the launch traced here: 207 us
  waiting for transfers between devices  101 us (49%)
  local copies, waits for them, and re-layouts  25 us (12%)
  matrix products  20.8 us (10%)
  other arithmetic  16.6 us (8%)
  starting transfers between devices  15.1 us (7%)
  between operations  14.1 us (7%)
  blocking collectives  13.9 us (7%)
    all_to_all x1, waiting for transfers between devices, body(): lax.all_to_all(jnp.stack([moved_k] * lax.axis_size('seq')), 'seq', 0, 0)  82.4 us
    all_gather x1, waiting for transfers between devices, body(): lax.all_gather(cross_v, ('seq', 'sub'), axis=0, tiled=True)  16.1 us
    reduce_sum x9, other arithmetic, absorb(): summed = summed * shrink + jnp.sum(weights, axis=2)  14.6 us
    dot_general x9, matrix products, absorb(): jnp.einsum('qhe,khe->hqk', queries.reshape(query_count, head_count, head_...  12.6 us
    dynamic_slice x12, local copies, waits for them, and re-layouts, fold_keys(): result, unused = lax.scan(one_block, state_in, (key_blocks, value_blocks))  8.35 us
    dot_general x9, matrix products, absorb(): jnp.einsum('hqk,khe->hqe', weights.astype(jnp.bfloat16), value_rows.resha...  8.23 us
    while x28, local copies, waits for them, and re-layouts  7.42 us
    all_to_all x1, starting transfers between devices, body(): lax.all_to_all(jnp.stack([moved_k] * lax.axis_size('seq')), 'seq', 0, 0)  6.48 us
  transfers between devices with their start and end apart: 7, of which 3 were waited for; matrix products, arithmetic and copies ran while one was open for 22% of the time, Pallas kernels for 0%

profile of v1, /device:TPU:0, one launch (start us, length us, event | category | flops | bytes accessed | tf_op | source)
XLA Modules:
  0.0 207.0 jit_solution(1417688503916554767)
XLA Ops:
  7.2 1.1 copy.136
  8.4 5.2 %all_to_all.75 = bf16[160,2,1024]{2,0,1:T(8,128)(2,1)} all-to-all(bf16[160,2,1024]{2,0,1:T(8,128)(2,1)S(1)} %bitcast.130), channel_id=1, replica_groups=mesh['grp'=2,'seq'=4,'head'=2,'sub'=2] {'sub'}, dimensions={1} | all-to-all | bytes 1310720 | tf_op jit(solution)/shard_map/all_to_all | solution.py:101
  13.6 0.7 all-gather.6.cloned.1.call-update
  14.3 0.9 copy.138
  15.2 3.5 %all-to-all-start = ((bf16[160,2,1024]{2,0,1:T(8,128)(2,1)}), bf16[160,2,1024]{2,0,1:T(8,128)(2,1)S(1)}, u32[]{:S(2)}, u32[]{:S(2)}) async-start(bf16[160,2,1024]{2,0,1:T(8,128)(2,1)} %bitcast.94), calls=%async_computation | async-start | bytes 1310720 | tf_op jit(solution)/shard_map/all_to_all | solution.py:100
  18.8 1.8 all-to-all-done
  20.6 4.2 %all_to_all.76 = bf16[160,2,1024]{2,0,1:T(8,128)(2,1)S(1)} all-to-all(bf16[160,2,1024]{2,0,1:T(8,128)(2,1)S(1)} %bitcast.128), channel_id=1, replica_groups=mesh['grp'=2,'seq'=4,'head'=2,'sub'=2] {'sub'}, dimensions={1} | all-to-all | bytes 1310720 | tf_op jit(solution)/shard_map/all_to_all | solution.py:99
  24.8 1.9 stack.10
  26.7 6.5 %all-to-all-start.1 = ((bf16[4,320,1024]{2,1,0:T(8,128)(2,1)}), bf16[4,320,1024]{2,1,0:T(8,128)(2,1)}, u32[]{:S(2)}, u32[]{:S(2)}) async-start(bf16[4,320,1024]{2,1,0:T(8,128)(2,1)} %stack.10), calls=%async_computation.1 | async-start | bytes 5242880 | tf_op jit(solution)/shard_map/all_to_all | solution.py:109
  33.2 1.3 collective-permute-start.1
  34.5 3.7 %collective-permute-start = (bf16[40,2048]{1,0:T(8,128)(2,1)S(1)}, bf16[40,2048]{1,0:T(8,128)(2,1)}, u32[]{:S(2)}, u32[]{:S(2)}) collective-permute-start(bf16[40,2048]{1,0:T(8,128)(2,1)S(1)} %constant_dynamic-update-slice_fusion), channel_id=1, source_target_pairs={{0,1},{1,4},{4,5},{5,8},{8,9},{9,12},{12,13},{2,3},{3,6},{6,7},{7,... | collective-permute-start | bytes 491528 | tf_op jit(solution)/shard_map/ppermute | solution.py:22
  38.8 1.0 pad_maximum_fusion
  39.9 0.8 copy.104
  40.9 0.9 fusion.37
  41.7 1.0 fusion.29
  42.8 0.6 fusion.28
  43.5 0.9 copy.105
  44.4 82.4 %all-to-all-done.1 = bf16[4,320,1024]{2,1,0:T(8,128)(2,1)} async-done(((bf16[4,320,1024]{2,1,0:T(8,128)(2,1)}), bf16[4,320,1024]{2,1,0:T(8,128)(2,1)}, u32[]{:S(2)}, u32[]{:S(2)}) %all-to-all-start.1) | async-done | bytes 2621472 | tf_op jit(solution)/shard_map/all_to_all | solution.py:109
  126.8 35.6 %while.30 = (s32[]{:T(128)}, f32[8,320]{1,0:T(8,128)S(1)}, f32[8,320]{1,0:T(8,128)S(1)}, f32[8,320,128]{2,1,0:T(8,128)S(1)}, bf16[4,320,1024]{2,1,0:T(8,128)(2,1...) while((s32[]{:T(128)}, f32[8,320]{1,0:T(8,128)S(1)}, ...), condition=%wide.region_3.4_spmd.clone, body=%wide.region_0.3_spmd.clone.sunk | while | flops 426979840 | bytes 32931984 | solution.py:83
  126.8 1.4 dynamic-slice_bitcast_fusion.3
  128.3 2.5 %bitcast_reduce_fusion.2 = (f32[8,320]{1,0:T(8,128)S(1)}, f32[8,320,320]{2,1,0:T(8,128)}) fusion(bf16[320,8,128]{2,1,0:T(8,128)(2,1)S(1)} %bitcast.122, bf16[320,1024]{1,0:T(8,128)(2,1)S(1)} %get-tuple-element.365), kind=kOutput, calls=%fused_computation.1.clone.1 | convolution fusion | flops 211351040 | bytes 4597760 | tf_op jit(solution)/shard_map/while/body/eval_jaxpr/qhe,khe->hqk/dot_general | solution.py:44
  130.9 3.0 %fusion.59 = f32[8,320]{1,0:T(8,128)S(1)} fusion(f32[8,320,320]{2,1,0:T(8,128)} %get-tuple-element.325, f32[8,320]{1,0:T(8,128)S(1)} %select_maximum_fusion.4), kind=kLoop, calls=%fused_computation.4.clone.1 | loop fusion | flops 2455040 | bytes 3297280 | tf_op jit(solution)/shard_map/while/body/eval_jaxpr/reduce_sum | solution.py:57
  134.2 1.4 fusion.61
  135.6 1.4 dynamic-slice_bitcast_fusion.3
  137.1 2.5 %bitcast_reduce_fusion.2 = (f32[8,320]{1,0:T(8,128)S(1)}, f32[8,320,320]{2,1,0:T(8,128)}) fusion(bf16[320,8,128]{2,1,0:T(8,128)(2,1)S(1)} %bitcast.122, bf16[320,1024]{1,0:T(8,128)(2,1)S(1)} %get-tuple-element.365), kind=kOutput, calls=%fused_computation.1.clone.1 | convolution fusion | flops 211351040 | bytes 4597760 | tf_op jit(solution)/shard_map/while/body/eval_jaxpr/qhe,khe->hqk/dot_general | solution.py:44
  139.6 3.0 %fusion.59 = f32[8,320]{1,0:T(8,128)S(1)} fusion(f32[8,320,320]{2,1,0:T(8,128)} %get-tuple-element.325, f32[8,320]{1,0:T(8,128)S(1)} %select_maximum_fusion.4), kind=kLoop, calls=%fused_computation.4.clone.1 | loop fusion | flops 2455040 | bytes 3297280 | tf_op jit(solution)/shard_map/while/body/eval_jaxpr/reduce_sum | solution.py:57
  143.0 1.4 fusion.61
  144.4 1.4 dynamic-slice_bitcast_fusion.3
  145.9 2.5 %bitcast_reduce_fusion.2 = (f32[8,320]{1,0:T(8,128)S(1)}, f32[8,320,320]{2,1,0:T(8,128)}) fusion(bf16[320,8,128]{2,1,0:T(8,128)(2,1)S(1)} %bitcast.122, bf16[320,1024]{1,0:T(8,128)(2,1)S(1)} %get-tuple-element.365), kind=kOutput, calls=%fused_computation.1.clone.1 | convolution fusion | flops 211351040 | bytes 4597760 | tf_op jit(solution)/shard_map/while/body/eval_jaxpr/qhe,khe->hqk/dot_general | solution.py:44
  148.5 3.0 %fusion.59 = f32[8,320]{1,0:T(8,128)S(1)} fusion(f32[8,320,320]{2,1,0:T(8,128)} %get-tuple-element.325, f32[8,320]{1,0:T(8,128)S(1)} %select_maximum_fusion.4), kind=kLoop, calls=%fused_computation.4.clone.1 | loop fusion | flops 2455040 | bytes 3297280 | tf_op jit(solution)/shard_map/while/body/eval_jaxpr/reduce_sum | solution.py:57
  151.8 1.4 fusion.61
  153.2 1.4 dynamic-slice_bitcast_fusion.3
  154.7 2.5 %bitcast_reduce_fusion.2 = (f32[8,320]{1,0:T(8,128)S(1)}, f32[8,320,320]{2,1,0:T(8,128)}) fusion(bf16[320,8,128]{2,1,0:T(8,128)(2,1)S(1)} %bitcast.122, bf16[320,1024]{1,0:T(8,128)(2,1)S(1)} %get-tuple-element.365), kind=kOutput, calls=%fused_computation.1.clone.1 | convolution fusion | flops 211351040 | bytes 4597760 | tf_op jit(solution)/shard_map/while/body/eval_jaxpr/qhe,khe->hqk/dot_general | solution.py:44
  157.3 3.1 %fusion.59 = f32[8,320]{1,0:T(8,128)S(1)} fusion(f32[8,320,320]{2,1,0:T(8,128)} %get-tuple-element.325, f32[8,320]{1,0:T(8,128)S(1)} %select_maximum_fusion.4), kind=kLoop, calls=%fused_computation.4.clone.1 | loop fusion | flops 2455040 | bytes 3297280 | tf_op jit(solution)/shard_map/while/body/eval_jaxpr/reduce_sum | solution.py:57
  161.0 1.4 fusion.61
  163.5 4.5 %all_to_all.77 = bf16[2,160,1024]{2,1,0:T(8,128)(2,1)S(1)} all-to-all(bf16[2,160,1024]{2,1,0:T(8,128)(2,1)S(1)} %convert_element_type.36), channel_id=1, replica_groups=mesh['grp'=2,'seq'=4,'head'=2,'sub'=2] {'sub'}, dimensions={0} | all-to-all | bytes 1310720 | tf_op jit(solution)/shard_map/all_to_all | solution.py:115
  168.0 0.9 copy.116
  168.9 16.1 %all-gather.8.cloned.1.call-done = bf16[1280,1024]{1,0:T(8,128)(2,1)} async-done(((bf16[160,1024]{1,0:T(8,128)(2,1)}), bf16[1280,1024]{1,0:T(8,128)(2,1)}) %all-gather.8.cloned.1.call-update) | async-done | bytes 2621456 | tf_op jit(solution)/shard_map/all_gather | solution.py:123
  185.0 14.4 %while.31 = (s32[]{:T(128)}, f32[16,40]{1,0:T(8,128)S(1)}, f32[16,40]{1,0:T(8,128)S(1)}, f32[16,40,64]{2,1,0:T(8,128)S(1)}, bf16[4,320,1024]{2,1,0:T(8,128)(2,1)...) while((s32[]{:T(128)}, f32[16,40]{1,0:T(8,128)S(1)}, ...), condition=%wide.region_7.8_spmd.clone, body=%wide.region_4.7_spmd.clone.sunk | while | flops 53783680 | bytes 9625717 | solution.py:83
  185.0 1.4 constant_dynamic-slice_fusion.3
  188.1 0.5 convolution_add_fusion.2
  188.6 1.4 constant_dynamic-slice_fusion.3
  191.7 0.5 convolution_add_fusion.2
  192.2 1.4 constant_dynamic-slice_fusion.3
  195.3 0.5 convolution_add_fusion.2
  195.8 1.4 constant_dynamic-slice_fusion.3
  198.9 0.5 convolution_add_fusion.2
  199.6 0.8 convert_element_type.39
  (109 shorter events, 10.8 us)
Async XLA Ops:
  7.2 119.6 %all-gather.4.cloned.1.call-start = ((), (), s32[]{:S(2)}) async-start(), calls=%async_computation.5 | async-start | bytes 3276800 | tf_op jit(solution)/shard_map/all_gather | solution.py:111
  8.3 6.0 %copy-start.2 = (bf16[160,2048]{1,0:T(8,128)(2,1)S(1)}, bf16[160,2048]{1,0:T(8,128)(2,1)}, u32[]{:S(2)}) copy-start(bf16[160,2048]{1,0:T(8,128)(2,1)} %param.15) | copy-start | bytes 1966084
  13.6 155.3 %all-gather.6.cloned.1.call-start = ((), (), s32[]{:S(2)}) async-start(), calls=%async_computation.6 | async-start | bytes 2949120 | tf_op jit(solution)/shard_map/all_gather | solution.py:122
  14.3 4.4 %copy-start.3 = (bf16[160,2048]{1,0:T(8,128)(2,1)S(1)}, bf16[160,2048]{1,0:T(8,128)(2,1)}, u32[]{:S(2)}) copy-start(bf16[160,2048]{1,0:T(8,128)(2,1)} %param.14) | copy-start | bytes 1966084
  15.2 5.3 %all-to-all-start = ((bf16[160,2,1024]{2,0,1:T(8,128)(2,1)}), bf16[160,2,1024]{2,0,1:T(8,128)(2,1)S(1)}, u32[]{:S(2)}, u32[]{:S(2)}) async-start(bf16[160,2,1024]{2,0,1:T(8,128)(2,1)} %bitcast.94), calls=%async_computation | async-start | bytes 1310720 | tf_op jit(solution)/shard_map/all_to_all | solution.py:100
  26.7 6.5 %copy-start.6 = (bf16[40,1024]{1,0:T(8,128)(2,1)S(1)}, bf16[40,1024]{1,0:T(8,128)(2,1)}, u32[]{:S(2)}) copy-start(bf16[40,1024]{1,0:T(8,128)(2,1)} %param.21) | copy-start | bytes 245764
  26.7 6.5 %copy-start.7 = (bf16[40,1024]{1,0:T(8,128)(2,1)S(1)}, bf16[40,1024]{1,0:T(8,128)(2,1)}, u32[]{:S(2)}) copy-start(bf16[40,1024]{1,0:T(8,128)(2,1)} %param.22) | copy-start | bytes 245764
  26.7 11.6 %copy-start.4 = (bf16[160,1024]{1,0:T(8,128)(2,1)S(1)}, bf16[160,1024]{1,0:T(8,128)(2,1)}, u32[]{:S(2)}) copy-start(bf16[160,1024]{1,0:T(8,128)(2,1)} %param.20) | copy-start | bytes 983044
  26.7 100.1 %all-to-all-start.1 = ((bf16[4,320,1024]{2,1,0:T(8,128)(2,1)}), bf16[4,320,1024]{2,1,0:T(8,128)(2,1)}, u32[]{:S(2)}, u32[]{:S(2)}) async-start(bf16[4,320,1024]{2,1,0:T(8,128)(2,1)} %stack.10), calls=%async_computation.1 | async-start | bytes 5242880 | tf_op jit(solution)/shard_map/all_to_all | solution.py:109
  33.1 5.4 %copy-start.8 = (s32[2,40]{1,0:T(2,128)S(1)}, s32[2,40]{1,0:T(2,128)}, u32[]{:S(2)}) copy-start(s32[2,40]{1,0:T(2,128)} %param.23) | copy-start | bytes 964
  33.1 151.8 %all-gather.8.cloned.1.call-start = ((), (), s32[]{:S(2)}) async-start(), calls=%async_computation.7 | async-start | bytes 2949120 | tf_op jit(solution)/shard_map/all_gather | solution.py:123
  33.2 5.6 %collective-permute-start.1 = (bf16[40,2048]{1,0:T(8,128)(2,1)S(1)}, bf16[40,2048]{1,0:T(8,128)(2,1)}, u32[]{:S(2)}, u32[]{:S(2)}) collective-permute-start(bf16[40,2048]{1,0:T(8,128)(2,1)S(1)} %constant_dynamic-update-slice_fusion), channel_id=1, source_target_pairs={{1,0},{4,1},{5,4},{8,5},{9,8},{12,9},{13,12},{3,2},{6,3},{7,6},{10... | collective-permute-start | bytes 491528 | tf_op jit(solution)/shard_map/ppermute | solution.py:24
  34.5 4.3 %collective-permute-start = (bf16[40,2048]{1,0:T(8,128)(2,1)S(1)}, bf16[40,2048]{1,0:T(8,128)(2,1)}, u32[]{:S(2)}, u32[]{:S(2)}) collective-permute-start(bf16[40,2048]{1,0:T(8,128)(2,1)S(1)} %constant_dynamic-update-slice_fusion), channel_id=1, source_target_pairs={{0,1},{1,4},{4,5},{5,8},{8,9},{9,12},{12,13},{2,3},{3,6},{6,7},{7,... | collective-permute-start | bytes 491528 | tf_op jit(solution)/shard_map/ppermute | solution.py:22
  40.9 1.9 copy-start.5
  130.9 3.3 %copy-start = (f32[8,320,320]{2,1,0:T(8,128)S(1)}, f32[8,320,320]{2,1,0:T(8,128)}, u32[]{:S(2)}) copy-start(f32[8,320,320]{2,1,0:T(8,128)} %get-tuple-element.325) | copy-start | bytes 9830404 | tf_op jit(solution)/shard_map/while
  139.6 3.4 %copy-start = (f32[8,320,320]{2,1,0:T(8,128)S(1)}, f32[8,320,320]{2,1,0:T(8,128)}, u32[]{:S(2)}) copy-start(f32[8,320,320]{2,1,0:T(8,128)} %get-tuple-element.325) | copy-start | bytes 9830404 | tf_op jit(solution)/shard_map/while
  148.5 3.3 %copy-start = (f32[8,320,320]{2,1,0:T(8,128)S(1)}, f32[8,320,320]{2,1,0:T(8,128)}, u32[]{:S(2)}) copy-start(f32[8,320,320]{2,1,0:T(8,128)} %get-tuple-element.325) | copy-start | bytes 9830404 | tf_op jit(solution)/shard_map/while
  157.3 3.7 %copy-start = (f32[8,320,320]{2,1,0:T(8,128)S(1)}, f32[8,320,320]{2,1,0:T(8,128)}, u32[]{:S(2)}) copy-start(f32[8,320,320]{2,1,0:T(8,128)} %get-tuple-element.325) | copy-start | bytes 9830404 | tf_op jit(solution)/shard_map/while
  163.5 21.5 %copy-start.1 = (bf16[40,1024]{1,0:T(8,128)(2,1)S(1)}, bf16[40,1024]{1,0:T(8,128)(2,1)}, u32[]{:S(2)}) copy-start(bf16[40,1024]{1,0:T(8,128)(2,1)} %param.17) | copy-start | bytes 245764
Sparse Core Ops, SparseCore 0:
  13.7 102.3 all-gather.3
  117.7 33.2 all-gather.5
  152.7 32.2 all-gather.7
